TPU v7x, 128 devices: a whole 4x4x4 slice. The times are simulated.
128 devices in a mesh: rows: 32 (over y_hi, z, x), batch: 4 (over y_lo, core).
Axes of the slice: x: 4, y: 4 (y_hi: 2, y_lo: 2; y = y_hi * 2 + y_lo), z: 4, core: 2. Of those that a mesh axis runs over, the one named last changes fastest.
Arguments:
- features: bfloat16 [4, 256, 128, 256], P('batch', 'rows'), may hold values from -6 to 6
- kernels: bfloat16 [3, 3, 3, 256, 256], replicated, may hold values from -0.125 to 0.125
- cotangent: bfloat16 [4, 256, 128, 256], P('batch', 'rows'), may hold values from -6 to 6
Outputs:
- result: bfloat16 [4, 256, 128, 256], P('batch', 'rows')
- grad_features: bfloat16 [4, 256, 128, 256], P('batch', 'rows')
- grad_kernels: float32 [3, 3, 3, 256, 256], replicated
All inputs are finite; a program needn't handle non-finite values.
Results may differ from a plain program's by a relative error of at most 0.0065.
Values may be sent and summed in bfloat16 or wider, within the bound.
No kernel may reach another device: no remote copies, remote signals or barrier semaphores. Data moves between devices by JAX's collectives and lax.ppermute only.
A program may use at most 128 MiB of HBM per device.

v0:
```python
import math
import jax
import jax.numpy as jnp
from jax import lax
from jax.sharding import PartitionSpec as P


def passed_along(value, axis, steps):
    count = lax.axis_size(axis)
    initial, last = (max(0, -steps), min(count, count - steps))
    return lax.ppermute(value, axis, [(source, source + steps) for source in range(initial, last)])


def activate(values):
    values = values.astype(jnp.float32)
    normed = values * lax.rsqrt(jnp.mean(values * values, axis=-1, keepdims=True) + 1e-05)
    return normed * jax.nn.sigmoid(normed)


def shift_columns(array, offset):
    width = array.shape[2]
    reach = abs(offset)
    padded = jnp.pad(array, ((0, 0), (0, 0), (reach, reach), (0, 0)))
    return padded[:, :, reach + offset : reach + offset + width]


def tap_forward(source, kernel_row, dilation):
    channels = kernel_row.shape[1]
    widened = jnp.transpose(kernel_row, (1, 0, 2)).reshape(channels, 3 * channels)
    product = jnp.einsum("shwc,cd->shwd", source, widened, preferred_element_type=jnp.float32)
    total = shift_columns(product[..., 0:channels], -dilation)
    total = total + product[..., channels : 2 * channels]
    return total + shift_columns(product[..., 2 * channels :], dilation)


def tap_backward(source, kernel_row, dilation):
    channels = kernel_row.shape[1]
    widened = jnp.transpose(kernel_row, (2, 0, 1)).reshape(channels, 3 * channels)
    product = jnp.einsum("shwd,dc->shwc", source, widened, preferred_element_type=jnp.float32)
    total = shift_columns(product[..., 0:channels], dilation)
    total = total + product[..., channels : 2 * channels]
    return total + shift_columns(product[..., 2 * channels :], -dilation)


def kernel_terms(source, grad_flow, dilation):
    channels = grad_flow.shape[3]
    stacked = jnp.concatenate(
        [shift_columns(grad_flow, dilation), grad_flow, shift_columns(grad_flow, -dilation)], axis=3
    )
    terms = jnp.einsum("shwc,shwd->cd", source, stacked, preferred_element_type=jnp.float32)
    return jnp.transpose(terms.reshape(channels, 3, channels), (1, 0, 2))


def fetch_bands(signal, bands_away):
    upper_band = passed_along(signal, "rows", bands_away)
    lower_band = passed_along(signal, "rows", -bands_away)
    return (upper_band, lower_band)


def fetch_grads(grad_flow, bands_away):
    grad_upper = passed_along(grad_flow, "rows", bands_away)
    grad_lower = passed_along(grad_flow, "rows", -bands_away)
    return (grad_upper, grad_lower)


def local(features, kernels, cotangent):
    band_rows = features.shape[1]
    count = lax.axis_size("rows")
    spans = [4, 8, 16]
    current = features
    grad_flow = cotangent
    saved = []
    for layer in range(3):
        dilation = spans[layer] * band_rows
        signal = activate(current).astype(jnp.bfloat16)
        upper_band, lower_band = fetch_bands(signal, spans[layer])
        conv_out = tap_forward(signal, kernels[layer, 1], dilation)
        conv_out = conv_out + tap_forward(upper_band, kernels[layer, 0], dilation)
        conv_out = conv_out + tap_forward(lower_band, kernels[layer, 2], dilation)
        saved.append((current, signal, upper_band, lower_band))
        current = (current.astype(jnp.float32) + conv_out).astype(jnp.bfloat16)
    pixel_count = features.shape[0] * band_rows * features.shape[2] * count * lax.axis_size("batch")
    factor = 1.0 / math.sqrt(pixel_count)
    kernel_grads = [None, None, None]
    for layer in [2, 1, 0]:
        dilation = spans[layer] * band_rows
        layer_input, signal, upper_band, lower_band = saved[layer]
        grad_upper, grad_lower = fetch_grads(grad_flow, spans[layer])
        dsignal = tap_backward(grad_flow, kernels[layer, 1], dilation)
        dsignal = dsignal + tap_backward(grad_lower, kernels[layer, 0], dilation)
        dsignal = dsignal + tap_backward(grad_upper, kernels[layer, 2], dilation)
        local_grad = (
            jnp.stack(
                [
                    kernel_terms(upper_band, grad_flow, dilation),
                    kernel_terms(signal, grad_flow, dilation),
                    kernel_terms(lower_band, grad_flow, dilation),
                ]
            )
            * factor
        )
        kernel_grads[layer] = local_grad
        _, back = jax.vjp(activate, layer_input.astype(jnp.float32))
        (dinput,) = back(dsignal)
        grad_flow = (grad_flow.astype(jnp.float32) + dinput).astype(jnp.bfloat16)
    summed = lax.psum(jnp.stack(kernel_grads), ("rows", "batch"))
    return (current, grad_flow, summed)


def solution(mesh):
    placed = (P("batch", "rows", None, None), P(), P("batch", "rows", None, None))
    return jax.shard_map(
        local,
        mesh=mesh,
        in_specs=placed,
        out_specs=(P("batch", "rows", None, None), P("batch", "rows", None, None), P()),
        check_vma=False,
    )
```

profile of v0, /device:TPU:1, one launch (start us, length us, event | category | flops | bytes accessed | tf_op | source)
XLA Modules:
  0.0 324.4 jit_solution(16525500430960883256)
XLA Ops:
  8.5 2.2 fusion.33
  12.0 5.8 %collective-permute-start = (bf16[1,8,128,256]{3,2,1,0:T(8,128)(2,1)}, bf16[1,8,128,256]{3,2,1,0:T(8,128)(2,1)}, u32[]{:S(2)}, u32[]{:S(2)}) collective-permute-start(bf16[1,8,128,256]{3,2,1,0:T(8,128)(2,1)} %fusion.33), channel_id=1, source_target_pairs={{0,16},{4,20},{8,24},{12,28},{16,32},{20,36},{24,40},{28,44},{32,4... | collective-permute-start | bytes 1572872 | tf_op jit(solution)/shard_map/ppermute | solution.py:11
  17.8 6.7 %collective-permute-start.7 = (bf16[1,8,128,256]{3,2,1,0:T(8,128)(2,1)}, bf16[1,8,128,256]{3,2,1,0:T(8,128)(2,1)}, u32[]{:S(2)}, u32[]{:S(2)}) collective-permute-start(bf16[1,8,128,256]{3,2,1,0:T(8,128)(2,1)} %param.5), channel_id=1, source_target_pairs={{0,64},{4,68},{8,72},{12,76},{16,80},{20,84},{24,88},{28,92},{32,9... | collective-permute-start | bytes 1572872 | tf_op jit(solution)/shard_map/ppermute | solution.py:11
  25.8 3.5 %fusion.118 = (bf16[1,1,3,256,256]{4,3,2,1,0:T(8,128)(2,1)}, bf16[1,1,3,256,256]{4,3,2,1,0:T(8,128)(2,1)}, bf16[1,1,3,256,256]{4,3,2,1,0:T(8,128)(2,1)}, bf16[1,...) fusion(bf16[3,3,3,256,256]{4,3,2,1,0:T(8,128)(2,1)} %param.4), kind=kLoop, calls=%fused_computation.206 | loop fusion | bytes 7077888 | tf_op jit(solution)/shard_map/slice | solution.py:77
  30.2 1.8 convolution_bitcast_fusion.17
  32.1 2.7 convolution_bitcast_fusion.8
  34.8 2.1 copy.89
  36.9 1.6 fusion.128
  38.6 1.4 pad_maximum_fusion.1
  42.4 1.6 convolution_bitcast_fusion.15
  44.2 1.6 convolution_bitcast_fusion.16
  47.6 1.8 fusion.60
  51.1 5.5 %collective-permute-start.2 = (bf16[1,8,128,256]{3,2,1,0:T(8,128)(2,1)S(1)}, bf16[1,8,128,256]{3,2,1,0:T(8,128)(2,1)S(1)}, u32[]{:S(2)}, u32[]{:S(2)}) collective-permute-start(bf16[1,8,128,256]{3,2,1,0:T(8,128)(2,1)S(1)} %fusion.27), channel_id=1, source_target_pairs={{0,32},{4,36},{8,40},{12,44},{16,48},{20,52},{24,56},{28,60},{32,6... | collective-permute-start | bytes 1572872 | tf_op jit(solution)/shard_map/ppermute | solution.py:11
  57.2 1.6 convolution_bitcast_fusion.6
  59.9 1.6 convolution_bitcast_fusion.7
  61.5 3.9 %collective-permute-done.3 = bf16[1,8,128,256]{3,2,1,0:T(8,128)(2,1)S(1)} collective-permute-done((bf16[1,8,128,256]{3,2,1,0:T(8,128)(2,1)S(1)}, bf16[1,8,128,256]{3,2,1,0:T(8,128)(2,1)S(1)}, u32[]{:S(2)}, u32[]{:S(2)}) %collective-permute-start.3) | collective-permute-done | bytes 524320 | tf_op jit(solution)/shard_map/ppermute | solution.py:11
  66.2 13.0 %collective-permute-done.2 = bf16[1,8,128,256]{3,2,1,0:T(8,128)(2,1)S(1)} collective-permute-done((bf16[1,8,128,256]{3,2,1,0:T(8,128)(2,1)S(1)}, bf16[1,8,128,256]{3,2,1,0:T(8,128)(2,1)S(1)}, u32[]{:S(2)}, u32[]{:S(2)}) %collective-permute-start.2) | collective-permute-done | bytes 524320 | tf_op jit(solution)/shard_map/ppermute | solution.py:11
  80.6 2.1 fusion.73
  82.7 1.4 fusion.45
  85.4 7.1 %collective-permute-start.4 = (bf16[1,8,128,256]{3,2,1,0:T(8,128)(2,1)}, bf16[1,8,128,256]{3,2,1,0:T(8,128)(2,1)}, u32[]{:S(2)}, u32[]{:S(2)}) collective-permute-start(bf16[1,8,128,256]{3,2,1,0:T(8,128)(2,1)} %get-tuple-element.47), channel_id=1, source_target_pairs={{0,64},{4,68},{8,72},{12,76},{16,80},{20,84},{24,88},{28,92},{32,9... | collective-permute-start | bytes 1572872 | tf_op jit(solution)/shard_map/ppermute | solution.py:11
  92.5 6.4 %collective-permute-start.9 = (bf16[1,8,128,256]{3,2,1,0:T(8,128)(2,1)S(1)}, bf16[1,8,128,256]{3,2,1,0:T(8,128)(2,1)}, u32[]{:S(2)}, u32[]{:S(2)}) collective-permute-start(bf16[1,8,128,256]{3,2,1,0:T(8,128)(2,1)S(1)} %get-tuple-element.46), channel_id=1, source_target_pairs={{0,32},{4,36},{8,40},{12,44},{16,48},{20,52},{24,56},{28,60},{32,6... | collective-permute-start | bytes 1572872 | tf_op jit(solution)/shard_map/ppermute | solution.py:11
  98.9 1.5 collective-permute-start.8
  100.5 2.3 convolution_bitcast_fusion.5
  102.8 2.5 convolution_bitcast_fusion.19
  106.6 3.0 copy.82
  109.6 3.1 convolution_bitcast_fusion.22
  112.7 1.5 convolution_bitcast_fusion.21
  115.9 1.5 convolution_bitcast_fusion.23
  117.5 2.1 collective-permute-done.9
  119.5 1.6 convolution_bitcast_fusion.3
  122.2 1.6 convolution_bitcast_fusion.4
  126.8 2.9 copy.75
  129.7 2.3 convolution_bitcast_fusion.25
  132.0 1.7 convolution_bitcast_fusion.18
  133.7 1.7 convolution_bitcast_fusion.20
  136.9 1.7 convolution_bitcast_fusion.24
  138.6 1.8 convolution_bitcast_fusion.26
  140.9 3.4 %pad_maximum_fusion = f32[3,3,3,256,256]{4,3,2,1,0:T(8,128)} fusion(f32[1,3,3,256,256]{4,3,2,1,0:T(8,128)S(1)} %maximum_multiply_fusion.2, f32[1,3,3,256,256]{4,3,2,1,0:T(8,128)S(1)} %get-tuple-element.53, f32[1,3,3,256,256]{4,3,2,1,0:T(8,128)S(1)} %get-tuple-element.52), kind=kLoop, calls=%fused_computation | loop fusion | flops 3538944 | bytes 14155776 | tf_op jit(solution)/shard_map/stack | solution.py:106
  144.4 2.0 copy.167
  148.2 1.8 convolution_bitcast_fusion.11
  150.0 1.6 collective-permute-start.11
  151.6 1.5 collective-permute-start.10
  154.9 1.7 convolution_bitcast_fusion.9
  156.6 1.6 convolution_bitcast_fusion.10
  159.4 5.4 %collective-permute-done.11 = bf16[1,8,128,256]{3,2,1,0:T(8,128)(2,1)S(1)} collective-permute-done((bf16[1,8,128,256]{3,2,1,0:T(8,128)(2,1)S(1)}, bf16[1,8,128,256]{3,2,1,0:T(8,128)(2,1)S(1)}, u32[]{:S(2)}, u32[]{:S(2)}) %collective-permute-start.11) | collective-permute-done | bytes 524320 | tf_op jit(solution)/shard_map/ppermute | solution.py:11
  165.3 5.2 %collective-permute-done.10 = bf16[1,8,128,256]{3,2,1,0:T(8,128)(2,1)S(1)} collective-permute-done((bf16[1,8,128,256]{3,2,1,0:T(8,128)(2,1)S(1)}, bf16[1,8,128,256]{3,2,1,0:T(8,128)(2,1)S(1)}, u32[]{:S(2)}, u32[]{:S(2)}) %collective-permute-start.10) | collective-permute-done | bytes 524320 | tf_op jit(solution)/shard_map/ppermute | solution.py:11
  173.8 137.1 %all-reduce.28.cloned.1.call-done = f32[3,3,3,256,256]{4,3,2,1,0:T(8,128)} async-done(((f32[3,3,3,256,256]{4,3,2,1,0:T(8,128)}), f32[3,3,3,256,256]{4,3,2,1,0:T(8,128)}) %all-reduce.28.cloned.1.call-update) | async-done | bytes 7077904 | tf_op jit(solution)/shard_map/psum | solution.py:106
  310.8 6.7 %copy.196 = f32[3,3,3,256,256]{4,3,2,1,0:T(8,128)} copy(f32[3,3,3,256,256]{4,3,2,1,0:T(8,128)} %all-reduce.28.cloned.1.call-done) | data formatting | bytes 14155776
  (139 shorter events, 33.3 us)
Async XLA Ops:
  7.2 303.7 %all-reduce.28.cloned.1.call-start = ((), (), s32[]{:S(2)}) async-start(), calls=%async_computation | async-start | bytes 14155776 | tf_op jit(solution)/shard_map/psum | solution.py:106
  10.7 31.7 %collective-permute-start.1 = (bf16[1,8,128,256]{3,2,1,0:T(8,128)(2,1)}, bf16[1,8,128,256]{3,2,1,0:T(8,128)(2,1)}, u32[]{:S(2)}, u32[]{:S(2)}) collective-permute-start(bf16[1,8,128,256]{3,2,1,0:T(8,128)(2,1)} %fusion.33), channel_id=1, source_target_pairs={{16,0},{20,4},{24,8},{28,12},{32,16},{36,20},{40,24},{44,28},{48,3... | collective-permute-start | bytes 1572872 | tf_op jit(solution)/shard_map/ppermute | solution.py:11
  12.0 32.3 %collective-permute-start = (bf16[1,8,128,256]{3,2,1,0:T(8,128)(2,1)}, bf16[1,8,128,256]{3,2,1,0:T(8,128)(2,1)}, u32[]{:S(2)}, u32[]{:S(2)}) collective-permute-start(bf16[1,8,128,256]{3,2,1,0:T(8,128)(2,1)} %fusion.33), channel_id=1, source_target_pairs={{0,16},{4,20},{8,24},{12,28},{16,32},{20,36},{24,40},{28,44},{32,4... | collective-permute-start | bytes 1572872 | tf_op jit(solution)/shard_map/ppermute | solution.py:11
  17.8 39.4 %collective-permute-start.7 = (bf16[1,8,128,256]{3,2,1,0:T(8,128)(2,1)}, bf16[1,8,128,256]{3,2,1,0:T(8,128)(2,1)}, u32[]{:S(2)}, u32[]{:S(2)}) collective-permute-start(bf16[1,8,128,256]{3,2,1,0:T(8,128)(2,1)} %param.5), channel_id=1, source_target_pairs={{0,64},{4,68},{8,72},{12,76},{16,80},{20,84},{24,88},{28,92},{32,9... | collective-permute-start | bytes 1572872 | tf_op jit(solution)/shard_map/ppermute | solution.py:11
  24.5 34.6 %collective-permute-start.6 = (bf16[1,8,128,256]{3,2,1,0:T(8,128)(2,1)}, bf16[1,8,128,256]{3,2,1,0:T(8,128)(2,1)}, u32[]{:S(2)}, u32[]{:S(2)}) collective-permute-start(bf16[1,8,128,256]{3,2,1,0:T(8,128)(2,1)} %param.5), channel_id=1, source_target_pairs={{64,0},{68,4},{72,8},{76,12},{80,16},{84,20},{88,24},{92,28},{96,3... | collective-permute-start | bytes 1572872 | tf_op jit(solution)/shard_map/ppermute | solution.py:11
  30.2 1.9 copy-start.3
  30.2 1.9 copy-start.10
  32.0 4.9 %copy-start.2 = (f32[1,8,128,768]{3,2,1,0:T(8,128)}, f32[1,8,128,768]{3,2,1,0:T(8,128)S(1)}, u32[]{:S(2)}) copy-start(f32[1,8,128,768]{3,2,1,0:T(8,128)S(1)} %convolution_bitcast_fusion.17) | copy-start | bytes 9437188
  36.9 1.7 copy-start.21
  38.5 1.5 copy-start.17
  38.5 2.4 copy-start.7
  38.6 2.7 copy-start.15
  38.6 3.6 %copy-start.19 = (bf16[1,1,3,256,256]{4,3,2,1,0:T(8,128)(2,1)S(1)}, bf16[1,1,3,256,256]{4,3,2,1,0:T(8,128)(2,1)}, u32[]{:S(2)}) copy-start(bf16[1,1,3,256,256]{4,3,2,1,0:T(8,128)(2,1)} %get-tuple-element.17) | copy-start | bytes 1179652
  45.9 1.0 copy-start
  45.9 1.4 copy-start.5
  45.9 1.7 copy-start.6
  49.4 7.9 %copy-start.14 = (bf16[1,1,3,256,256]{4,3,2,1,0:T(8,128)(2,1)S(1)}, bf16[1,1,3,256,256]{4,3,2,1,0:T(8,128)(2,1)}, u32[]{:S(2)}) copy-start(bf16[1,1,3,256,256]{4,3,2,1,0:T(8,128)(2,1)} %get-tuple-element.21) | copy-start | bytes 1179652
  49.7 9.1 %copy-start.22 = (bf16[1,8,128,256]{3,2,1,0:T(8,128)(2,1)}, bf16[1,8,128,256]{3,2,1,0:T(8,128)(2,1)S(1)}, u32[]{:S(2)}) copy-start(bf16[1,8,128,256]{3,2,1,0:T(8,128)(2,1)S(1)} %fusion.27) | copy-start | bytes 1572868
  49.8 15.7 %collective-permute-start.3 = (bf16[1,8,128,256]{3,2,1,0:T(8,128)(2,1)S(1)}, bf16[1,8,128,256]{3,2,1,0:T(8,128)(2,1)S(1)}, u32[]{:S(2)}, u32[]{:S(2)}) collective-permute-start(bf16[1,8,128,256]{3,2,1,0:T(8,128)(2,1)S(1)} %fusion.27), channel_id=1, source_target_pairs={{32,0},{36,4},{40,8},{44,12},{48,16},{52,20},{56,24},{60,28},{64,3... | collective-permute-start | bytes 1572872 | tf_op jit(solution)/shard_map/ppermute | solution.py:11
  51.1 28.2 %collective-permute-start.2 = (bf16[1,8,128,256]{3,2,1,0:T(8,128)(2,1)S(1)}, bf16[1,8,128,256]{3,2,1,0:T(8,128)(2,1)S(1)}, u32[]{:S(2)}, u32[]{:S(2)}) collective-permute-start(bf16[1,8,128,256]{3,2,1,0:T(8,128)(2,1)S(1)} %fusion.27), channel_id=1, source_target_pairs={{0,32},{4,36},{8,40},{12,44},{16,48},{20,52},{24,56},{28,60},{32,6... | collective-permute-start | bytes 1572872 | tf_op jit(solution)/shard_map/ppermute | solution.py:11
  59.0 6.4 %copy-start.29 = (bf16[1,1,3,256,256]{3,4,2,1,0:T(8,128)(2,1)S(1)}, bf16[1,1,3,256,256]{3,4,2,1,0:T(8,128)(2,1)}, u32[]{:S(2)}) copy-start(bf16[1,1,3,256,256]{3,4,2,1,0:T(8,128)(2,1)} %copy.164) | copy-start | bytes 1179652
  66.0 13.2 %copy-start.28 = (bf16[1,1,3,256,256]{3,4,2,1,0:T(8,128)(2,1)S(1)}, bf16[1,1,3,256,256]{3,4,2,1,0:T(8,128)(2,1)}, u32[]{:S(2)}) copy-start(bf16[1,1,3,256,256]{3,4,2,1,0:T(8,128)(2,1)} %copy.163) | copy-start | bytes 1179652
  80.6 2.1 copy-start.4
  82.7 17.7 %copy-start.20 = (bf16[1,1,3,256,256]{4,3,2,1,0:T(8,128)(2,1)S(1)}, bf16[1,1,3,256,256]{4,3,2,1,0:T(8,128)(2,1)}, u32[]{:S(2)}) copy-start(bf16[1,1,3,256,256]{4,3,2,1,0:T(8,128)(2,1)} %get-tuple-element.17) | copy-start | bytes 1179652
  84.1 47.9 %collective-permute-start.5 = (bf16[1,8,128,256]{3,2,1,0:T(8,128)(2,1)}, bf16[1,8,128,256]{3,2,1,0:T(8,128)(2,1)}, u32[]{:S(2)}, u32[]{:S(2)}) collective-permute-start(bf16[1,8,128,256]{3,2,1,0:T(8,128)(2,1)} %get-tuple-element.47), channel_id=1, source_target_pairs={{64,0},{68,4},{72,8},{76,12},{80,16},{84,20},{88,24},{92,28},{96,3... | collective-permute-start | bytes 1572872 | tf_op jit(solution)/shard_map/ppermute | solution.py:11
  85.4 48.3 %collective-permute-start.4 = (bf16[1,8,128,256]{3,2,1,0:T(8,128)(2,1)}, bf16[1,8,128,256]{3,2,1,0:T(8,128)(2,1)}, u32[]{:S(2)}, u32[]{:S(2)}) collective-permute-start(bf16[1,8,128,256]{3,2,1,0:T(8,128)(2,1)} %get-tuple-element.47), channel_id=1, source_target_pairs={{0,64},{4,68},{8,72},{12,76},{16,80},{20,84},{24,88},{28,92},{32,9... | collective-permute-start | bytes 1572872 | tf_op jit(solution)/shard_map/ppermute | solution.py:11
  92.5 27.0 %collective-permute-start.9 = (bf16[1,8,128,256]{3,2,1,0:T(8,128)(2,1)S(1)}, bf16[1,8,128,256]{3,2,1,0:T(8,128)(2,1)}, u32[]{:S(2)}, u32[]{:S(2)}) collective-permute-start(bf16[1,8,128,256]{3,2,1,0:T(8,128)(2,1)S(1)} %get-tuple-element.46), channel_id=1, source_target_pairs={{0,32},{4,36},{8,40},{12,44},{16,48},{20,52},{24,56},{28,60},{32,6... | collective-permute-start | bytes 1572872 | tf_op jit(solution)/shard_map/ppermute | solution.py:11
  98.9 22.5 %collective-permute-start.8 = (bf16[1,8,128,256]{3,2,1,0:T(8,128)(2,1)S(1)}, bf16[1,8,128,256]{3,2,1,0:T(8,128)(2,1)}, u32[]{:S(2)}, u32[]{:S(2)}) collective-permute-start(bf16[1,8,128,256]{3,2,1,0:T(8,128)(2,1)S(1)} %get-tuple-element.46), channel_id=1, source_target_pairs={{32,0},{36,4},{40,8},{44,12},{48,16},{52,20},{56,24},{60,28},{64,3... | collective-permute-start | bytes 1572872 | tf_op jit(solution)/shard_map/ppermute | solution.py:11
  100.4 2.3 copy-start.24
  106.6 3.0 copy-start.23
  109.6 3.1 copy-start.27
  109.6 3.1 copy-start.39
  112.7 2.2 copy-start.1
  114.9 1.0 copy-start.37
  115.9 3.6 %copy-start.18 = (bf16[1,1,3,256,256]{4,3,2,1,0:T(8,128)(2,1)S(1)}, bf16[1,1,3,256,256]{4,3,2,1,0:T(8,128)(2,1)}, u32[]{:S(2)}) copy-start(bf16[1,1,3,256,256]{4,3,2,1,0:T(8,128)(2,1)} %get-tuple-element.15) | copy-start | bytes 1179652
  129.7 2.3 copy-start.25
  133.7 1.8 copy-start.34
  135.5 1.4 copy-start.26
  138.6 1.9 copy-start.32
  138.6 1.9 copy-start.33
  138.6 1.9 copy-start.35
  144.4 2.0 copy-start.13
  144.4 2.9 copy-start.11
  147.3 5.9 %copy-start.9 = (bf16[1,1,3,256,256]{4,3,2,1,0:T(8,128)(2,1)S(1)}, bf16[1,1,3,256,256]{4,3,2,1,0:T(8,128)(2,1)}, u32[]{:S(2)}) copy-start(bf16[1,1,3,256,256]{4,3,2,1,0:T(8,128)(2,1)} %copy-done.8) | copy-start | bytes 1179652
  150.0 14.7 %collective-permute-start.11 = (bf16[1,8,128,256]{3,2,1,0:T(8,128)(2,1)S(1)}, bf16[1,8,128,256]{3,2,1,0:T(8,128)(2,1)S(1)}, u32[]{:S(2)}, u32[]{:S(2)}) collective-permute-start(bf16[1,8,128,256]{3,2,1,0:T(8,128)(2,1)S(1)} %fusion.47), channel_id=1, source_target_pairs={{0,16},{4,20},{8,24},{12,28},{16,32},{20,36},{24,40},{28,44},{32,4... | collective-permute-start | bytes 1572872 | tf_op jit(solution)/shard_map/ppermute | solution.py:11
  151.6 18.9 %collective-permute-start.10 = (bf16[1,8,128,256]{3,2,1,0:T(8,128)(2,1)S(1)}, bf16[1,8,128,256]{3,2,1,0:T(8,128)(2,1)S(1)}, u32[]{:S(2)}, u32[]{:S(2)}) collective-permute-start(bf16[1,8,128,256]{3,2,1,0:T(8,128)(2,1)S(1)} %fusion.47), channel_id=1, source_target_pairs={{16,0},{20,4},{24,8},{28,12},{32,16},{36,20},{40,24},{44,28},{48,3... | collective-permute-start | bytes 1572872 | tf_op jit(solution)/shard_map/ppermute | solution.py:11
  153.8 1.1 copy-start.31
  154.0 2.6 copy-start.30
  (5 other events, 4.6 us)
Sparse Core Ops, SparseCore 0:
  144.5 166.2 all-reduce.27
where the time goes:
time: 326 us; the launch traced here: 324 us
  waiting for transfers between devices  167 us (51%)
  matrix products  43.3 us (13%)
  starting transfers between devices  41.3 us (13%)
  local copies, waits for them, and re-layouts  35.9 us (11%)
  other arithmetic  22.5 us (7%)
  between operations  14.8 us (5%)
    psum x1, waiting for transfers between devices, local(): summed = lax.psum(jnp.stack(kernel_grads), ('rows', 'batch'))  137 us
    ppermute x12, starting transfers between devices, passed_along(): lax.ppermute(value, axis, [(source, source + steps) for source in range(i...  41.3 us
    ppermute x12, waiting for transfers between devices, passed_along(): lax.ppermute(value, axis, [(source, source + steps) for source in range(i...  29.5 us
    unnamed x91, local copies, waits for them, and re-layouts  22.8 us
    dot_general x9, matrix products, kernel_terms(): jnp.einsum('shwc,shwd->cd', source, stacked, preferred_element_type=jnp.f...  17.9 us
    dot_general x9, matrix products, tap_backward(): jnp.einsum('shwd,dc->shwc', source, widened, preferred_element_type=jnp.f...  13.4 us
    dot_general x9, matrix products, tap_forward(): jnp.einsum('shwc,cd->shwd', source, widened, preferred_element_type=jnp.f...  12 us
  transfers between devices with their start and end apart: 13, of which 6 were waited for; matrix products, arithmetic and copies ran while one was open for 22% of the time, Pallas kernels for 0%

commit v1 on v0

--- a/solution.py
+++ b/solution.py
@@ -103,7 +103,7 @@
         _, back = jax.vjp(activate, layer_input.astype(jnp.float32))
         (dinput,) = back(dsignal)
         grad_flow = (grad_flow.astype(jnp.float32) + dinput).astype(jnp.bfloat16)
-    summed = lax.psum(jnp.stack(kernel_grads), ("rows", "batch"))
+    summed = lax.psum(lax.psum(jnp.stack(kernel_grads), "batch"), "rows")
     return (current, grad_flow, summed)
 
 

time: 326 us -> 683 us (2.10)
  the two profiles are of different devices: /device:TPU:1 before, /device:TPU:0 now
where the time goes in v1:
time: 683 us; the launch traced here: 681 us
  waiting for transfers between devices  521 us (76%)
  starting transfers between devices  44.5 us (7%)
  matrix products  43.2 us (6%)
  local copies, waits for them, and re-layouts  35.9 us (5%)
  other arithmetic  22.4 us (3%)
  between operations  14.8 us (2%)
    psum x2, waiting for transfers between devices, local(): summed = lax.psum(lax.psum(jnp.stack(kernel_grads), 'batch'), 'rows')  488 us
    ppermute x12, starting transfers between devices, passed_along(): lax.ppermute(value, axis, [(source, source + steps) for source in range(i...  44.5 us
    ppermute x12, waiting for transfers between devices, passed_along(): lax.ppermute(value, axis, [(source, source + steps) for source in range(i...  32.9 us
    unnamed x91, local copies, waits for them, and re-layouts  22.7 us
    dot_general x9, matrix products, kernel_terms(): jnp.einsum('shwc,shwd->cd', source, stacked, preferred_element_type=jnp.f...  17.8 us
  transfers between devices with their start and end apart: 14, of which 6 were waited for; matrix products, arithmetic and copies ran while one was open for 10% of the time, Pallas kernels for 0%

profile of v1, /device:TPU:0, one launch (start us, length us, event | category | flops | bytes accessed | tf_op | source)
XLA Modules:
  0.0 681.4 jit_solution(16347661668711821475)
XLA Ops:
  8.5 2.2 fusion.33
  12.0 5.4 collective-permute-start
  17.4 7.0 %collective-permute-start.7 = (bf16[1,8,128,256]{3,2,1,0:T(8,128)(2,1)}, bf16[1,8,128,256]{3,2,1,0:T(8,128)(2,1)}, u32[]{:S(2)}, u32[]{:S(2)}) collective-permute-start(bf16[1,8,128,256]{3,2,1,0:T(8,128)(2,1)} %param.5), channel_id=1, source_target_pairs={{0,64},{4,68},{8,72},{12,76},{16,80},{20,84},{24,88},{28,92},{32,9... | collective-permute-start | bytes 1572872 | tf_op jit(solution)/shard_map/ppermute | solution.py:11
  25.7 3.5 fusion.118
  30.1 1.8 convolution_bitcast_fusion.17
  32.0 2.6 convolution_bitcast_fusion.8
  34.7 2.1 copy.89
  36.8 1.5 fusion.128
  38.4 1.4 pad_maximum_fusion.1
  42.2 1.6 convolution_bitcast_fusion.15
  44.0 1.6 convolution_bitcast_fusion.16
  47.4 1.8 fusion.60
  50.9 6.1 collective-permute-start.2
  57.6 1.6 convolution_bitcast_fusion.6
  60.3 1.6 convolution_bitcast_fusion.7
  61.9 4.2 collective-permute-done.3
  66.9 11.3 %collective-permute-done.2 = bf16[1,8,128,256]{3,2,1,0:T(8,128)(2,1)S(1)} collective-permute-done((bf16[1,8,128,256]{3,2,1,0:T(8,128)(2,1)S(1)}, bf16[1,8,128,256]{3,2,1,0:T(8,128)(2,1)S(1)}, u32[]{:S(2)}, u32[]{:S(2)}) %collective-permute-start.2) | collective-permute-done | bytes 524320 | tf_op jit(solution)/shard_map/ppermute | solution.py:11
  79.6 2.1 fusion.73
  81.8 1.4 fusion.45
  84.5 8.8 %collective-permute-start.4 = (bf16[1,8,128,256]{3,2,1,0:T(8,128)(2,1)}, bf16[1,8,128,256]{3,2,1,0:T(8,128)(2,1)}, u32[]{:S(2)}, u32[]{:S(2)}) collective-permute-start(bf16[1,8,128,256]{3,2,1,0:T(8,128)(2,1)} %get-tuple-element.47), channel_id=1, source_target_pairs={{0,64},{4,68},{8,72},{12,76},{16,80},{20,84},{24,88},{28,92},{32,9... | collective-permute-start | bytes 1572872 | tf_op jit(solution)/shard_map/ppermute | solution.py:11
  93.2 5.6 collective-permute-start.9
  98.8 1.5 collective-permute-start.8
  100.4 2.3 convolution_bitcast_fusion.5
  102.7 2.6 convolution_bitcast_fusion.19
  106.5 3.0 copy.82
  109.5 3.1 convolution_bitcast_fusion.22
  112.5 1.5 convolution_bitcast_fusion.21
  115.7 1.5 convolution_bitcast_fusion.23
  117.3 2.8 collective-permute-done.9
  120.0 1.6 convolution_bitcast_fusion.3
  122.7 1.7 convolution_bitcast_fusion.4
  127.3 2.9 copy.75
  130.2 2.3 convolution_bitcast_fusion.25
  132.5 1.7 convolution_bitcast_fusion.18
  134.2 1.7 convolution_bitcast_fusion.20
  137.4 1.7 convolution_bitcast_fusion.24
  139.1 1.8 convolution_bitcast_fusion.26
  141.4 3.4 pad_maximum_fusion
  144.9 138.3 %all-reduce.29.cloned.1.call-done = f32[3,3,3,256,256]{4,3,2,1,0:T(8,128)} async-done(((f32[3,3,3,256,256]{4,3,2,1,0:T(8,128)}), f32[3,3,3,256,256]{4,3,2,1,0:T(8,128)}) %all-reduce.29.cloned.1.call-update) | async-done | bytes 7077904 | tf_op jit(solution)/shard_map/psum | solution.py:106
  283.2 2.0 copy.167
  287.1 1.8 convolution_bitcast_fusion.11
  288.8 3.5 collective-permute-start.11
  292.3 1.5 collective-permute-start.10
  295.5 1.7 convolution_bitcast_fusion.9
  297.1 1.6 convolution_bitcast_fusion.10
  299.9 14.6 %collective-permute-done.11 = bf16[1,8,128,256]{3,2,1,0:T(8,128)(2,1)S(1)} collective-permute-done((bf16[1,8,128,256]{3,2,1,0:T(8,128)(2,1)S(1)}, bf16[1,8,128,256]{3,2,1,0:T(8,128)(2,1)S(1)}, u32[]{:S(2)}, u32[]{:S(2)}) %collective-permute-start.11) | collective-permute-done | bytes 524320 | tf_op jit(solution)/shard_map/ppermute | solution.py:11
  318.5 349.4 %all-reduce.31.cloned.1.call-done = f32[3,3,3,256,256]{4,3,2,1,0:T(8,128)} async-done(((f32[3,3,3,256,256]{4,3,2,1,0:T(8,128)}), f32[3,3,3,256,256]{4,3,2,1,0:T(8,128)}) %all-reduce.31.cloned.1.call-update) | async-done | bytes 7077904 | tf_op jit(solution)/shard_map/psum | solution.py:106
  667.9 6.7 copy.197
  (142 shorter events, 33.2 us)
Async XLA Ops:
  7.2 276.0 %all-reduce.29.cloned.1.call-start = ((), (), s32[]{:S(2)}) async-start(), calls=%async_computation | async-start | bytes 14155776 | tf_op jit(solution)/shard_map/psum | solution.py:106
  10.7 31.5 %collective-permute-start.1 = (bf16[1,8,128,256]{3,2,1,0:T(8,128)(2,1)}, bf16[1,8,128,256]{3,2,1,0:T(8,128)(2,1)}, u32[]{:S(2)}, u32[]{:S(2)}) collective-permute-start(bf16[1,8,128,256]{3,2,1,0:T(8,128)(2,1)} %fusion.33), channel_id=1, source_target_pairs={{16,0},{20,4},{24,8},{28,12},{32,16},{36,20},{40,24},{44,28},{48,3... | collective-permute-start | bytes 1572872 | tf_op jit(solution)/shard_map/ppermute | solution.py:11
  12.0 32.1 %collective-permute-start = (bf16[1,8,128,256]{3,2,1,0:T(8,128)(2,1)}, bf16[1,8,128,256]{3,2,1,0:T(8,128)(2,1)}, u32[]{:S(2)}, u32[]{:S(2)}) collective-permute-start(bf16[1,8,128,256]{3,2,1,0:T(8,128)(2,1)} %fusion.33), channel_id=1, source_target_pairs={{0,16},{4,20},{8,24},{12,28},{16,32},{20,36},{24,40},{28,44},{32,4... | collective-permute-start | bytes 1572872 | tf_op jit(solution)/shard_map/ppermute | solution.py:11
  17.4 40.2 %collective-permute-start.7 = (bf16[1,8,128,256]{3,2,1,0:T(8,128)(2,1)}, bf16[1,8,128,256]{3,2,1,0:T(8,128)(2,1)}, u32[]{:S(2)}, u32[]{:S(2)}) collective-permute-start(bf16[1,8,128,256]{3,2,1,0:T(8,128)(2,1)} %param.5), channel_id=1, source_target_pairs={{0,64},{4,68},{8,72},{12,76},{16,80},{20,84},{24,88},{28,92},{32,9... | collective-permute-start | bytes 1572872 | tf_op jit(solution)/shard_map/ppermute | solution.py:11
  24.4 35.0 %collective-permute-start.6 = (bf16[1,8,128,256]{3,2,1,0:T(8,128)(2,1)}, bf16[1,8,128,256]{3,2,1,0:T(8,128)(2,1)}, u32[]{:S(2)}, u32[]{:S(2)}) collective-permute-start(bf16[1,8,128,256]{3,2,1,0:T(8,128)(2,1)} %param.5), channel_id=1, source_target_pairs={{64,0},{68,4},{72,8},{76,12},{80,16},{84,20},{88,24},{92,28},{96,3... | collective-permute-start | bytes 1572872 | tf_op jit(solution)/shard_map/ppermute | solution.py:11
  30.1 1.9 copy-start.3
  30.1 1.9 copy-start.10
  32.0 4.8 copy-start.2
  36.8 1.6 copy-start.21
  38.3 1.5 copy-start.17
  38.3 2.4 copy-start.7
  38.4 2.6 copy-start.15
  38.4 3.6 copy-start.19
  45.7 1.0 copy-start
  45.7 1.4 copy-start.5
  45.7 1.7 copy-start.6
  49.2 8.4 %copy-start.14 = (bf16[1,1,3,256,256]{4,3,2,1,0:T(8,128)(2,1)S(1)}, bf16[1,1,3,256,256]{4,3,2,1,0:T(8,128)(2,1)}, u32[]{:S(2)}) copy-start(bf16[1,1,3,256,256]{4,3,2,1,0:T(8,128)(2,1)} %get-tuple-element.21) | copy-start | bytes 1179652
  49.6 9.7 %copy-start.22 = (bf16[1,8,128,256]{3,2,1,0:T(8,128)(2,1)}, bf16[1,8,128,256]{3,2,1,0:T(8,128)(2,1)S(1)}, u32[]{:S(2)}) copy-start(bf16[1,8,128,256]{3,2,1,0:T(8,128)(2,1)S(1)} %fusion.27) | copy-start | bytes 1572868
  49.6 16.5 %collective-permute-start.3 = (bf16[1,8,128,256]{3,2,1,0:T(8,128)(2,1)S(1)}, bf16[1,8,128,256]{3,2,1,0:T(8,128)(2,1)S(1)}, u32[]{:S(2)}, u32[]{:S(2)}) collective-permute-start(bf16[1,8,128,256]{3,2,1,0:T(8,128)(2,1)S(1)} %fusion.27), channel_id=1, source_target_pairs={{32,0},{36,4},{40,8},{44,12},{48,16},{52,20},{56,24},{60,28},{64,3... | collective-permute-start | bytes 1572872 | tf_op jit(solution)/shard_map/ppermute | solution.py:11
  50.9 27.4 %collective-permute-start.2 = (bf16[1,8,128,256]{3,2,1,0:T(8,128)(2,1)S(1)}, bf16[1,8,128,256]{3,2,1,0:T(8,128)(2,1)S(1)}, u32[]{:S(2)}, u32[]{:S(2)}) collective-permute-start(bf16[1,8,128,256]{3,2,1,0:T(8,128)(2,1)S(1)} %fusion.27), channel_id=1, source_target_pairs={{0,32},{4,36},{8,40},{12,44},{16,48},{20,52},{24,56},{28,60},{32,6... | collective-permute-start | bytes 1572872 | tf_op jit(solution)/shard_map/ppermute | solution.py:11
  59.4 6.7 copy-start.29
  66.7 11.6 %copy-start.28 = (bf16[1,1,3,256,256]{3,4,2,1,0:T(8,128)(2,1)S(1)}, bf16[1,1,3,256,256]{3,4,2,1,0:T(8,128)(2,1)}, u32[]{:S(2)}) copy-start(bf16[1,1,3,256,256]{3,4,2,1,0:T(8,128)(2,1)} %copy.163) | copy-start | bytes 1179652
  79.6 2.1 copy-start.4
  81.8 18.6 %copy-start.20 = (bf16[1,1,3,256,256]{4,3,2,1,0:T(8,128)(2,1)S(1)}, bf16[1,1,3,256,256]{4,3,2,1,0:T(8,128)(2,1)}, u32[]{:S(2)}) copy-start(bf16[1,1,3,256,256]{4,3,2,1,0:T(8,128)(2,1)} %get-tuple-element.17) | copy-start | bytes 1179652
  83.2 49.4 %collective-permute-start.5 = (bf16[1,8,128,256]{3,2,1,0:T(8,128)(2,1)}, bf16[1,8,128,256]{3,2,1,0:T(8,128)(2,1)}, u32[]{:S(2)}, u32[]{:S(2)}) collective-permute-start(bf16[1,8,128,256]{3,2,1,0:T(8,128)(2,1)} %get-tuple-element.47), channel_id=1, source_target_pairs={{64,0},{68,4},{72,8},{76,12},{80,16},{84,20},{88,24},{92,28},{96,3... | collective-permute-start | bytes 1572872 | tf_op jit(solution)/shard_map/ppermute | solution.py:11
  84.5 49.8 %collective-permute-start.4 = (bf16[1,8,128,256]{3,2,1,0:T(8,128)(2,1)}, bf16[1,8,128,256]{3,2,1,0:T(8,128)(2,1)}, u32[]{:S(2)}, u32[]{:S(2)}) collective-permute-start(bf16[1,8,128,256]{3,2,1,0:T(8,128)(2,1)} %get-tuple-element.47), channel_id=1, source_target_pairs={{0,64},{4,68},{8,72},{12,76},{16,80},{20,84},{24,88},{28,92},{32,9... | collective-permute-start | bytes 1572872 | tf_op jit(solution)/shard_map/ppermute | solution.py:11
  93.2 26.8 %collective-permute-start.9 = (bf16[1,8,128,256]{3,2,1,0:T(8,128)(2,1)S(1)}, bf16[1,8,128,256]{3,2,1,0:T(8,128)(2,1)}, u32[]{:S(2)}, u32[]{:S(2)}) collective-permute-start(bf16[1,8,128,256]{3,2,1,0:T(8,128)(2,1)S(1)} %get-tuple-element.46), channel_id=1, source_target_pairs={{0,32},{4,36},{8,40},{12,44},{16,48},{20,52},{24,56},{28,60},{32,6... | collective-permute-start | bytes 1572872 | tf_op jit(solution)/shard_map/ppermute | solution.py:11
  98.8 23.1 %collective-permute-start.8 = (bf16[1,8,128,256]{3,2,1,0:T(8,128)(2,1)S(1)}, bf16[1,8,128,256]{3,2,1,0:T(8,128)(2,1)}, u32[]{:S(2)}, u32[]{:S(2)}) collective-permute-start(bf16[1,8,128,256]{3,2,1,0:T(8,128)(2,1)S(1)} %get-tuple-element.46), channel_id=1, source_target_pairs={{32,0},{36,4},{40,8},{44,12},{48,16},{52,20},{56,24},{60,28},{64,3... | collective-permute-start | bytes 1572872 | tf_op jit(solution)/shard_map/ppermute | solution.py:11
  100.3 2.3 copy-start.24
  106.5 3.0 copy-start.23
  109.4 3.1 copy-start.27
  109.4 3.1 copy-start.39
  112.5 2.2 copy-start.1
  114.7 1.0 copy-start.37
  115.7 4.3 copy-start.18
  130.2 2.3 copy-start.25
  134.2 1.8 copy-start.34
  136.0 1.4 copy-start.26
  139.1 1.9 copy-start.32
  139.1 1.9 copy-start.33
  139.1 1.9 copy-start.35
  144.9 523.0 %all-reduce.31.cloned.1.call-start = ((), (), s32[]{:S(2)}) async-start(), calls=%async_computation.1 | async-start | bytes 14155776 | tf_op jit(solution)/shard_map/psum | solution.py:106
  283.2 2.0 copy-start.13
  283.2 2.9 copy-start.11
  286.1 7.7 %copy-start.9 = (bf16[1,1,3,256,256]{4,3,2,1,0:T(8,128)(2,1)S(1)}, bf16[1,1,3,256,256]{4,3,2,1,0:T(8,128)(2,1)}, u32[]{:S(2)}) copy-start(bf16[1,1,3,256,256]{4,3,2,1,0:T(8,128)(2,1)} %copy-done.8) | copy-start | bytes 1179652
  288.8 25.7 %collective-permute-start.11 = (bf16[1,8,128,256]{3,2,1,0:T(8,128)(2,1)S(1)}, bf16[1,8,128,256]{3,2,1,0:T(8,128)(2,1)S(1)}, u32[]{:S(2)}, u32[]{:S(2)}) collective-permute-start(bf16[1,8,128,256]{3,2,1,0:T(8,128)(2,1)S(1)} %fusion.47), channel_id=1, source_target_pairs={{0,16},{4,20},{8,24},{12,28},{16,32},{20,36},{24,40},{28,44},{32,4... | collective-permute-start | bytes 1572872 | tf_op jit(solution)/shard_map/ppermute | solution.py:11
  292.3 22.8 %collective-permute-start.10 = (bf16[1,8,128,256]{3,2,1,0:T(8,128)(2,1)S(1)}, bf16[1,8,128,256]{3,2,1,0:T(8,128)(2,1)S(1)}, u32[]{:S(2)}, u32[]{:S(2)}) collective-permute-start(bf16[1,8,128,256]{3,2,1,0:T(8,128)(2,1)S(1)} %fusion.47), channel_id=1, source_target_pairs={{16,0},{20,4},{24,8},{28,12},{32,16},{36,20},{40,24},{44,28},{48,3... | collective-permute-start | bytes 1572872 | tf_op jit(solution)/shard_map/ppermute | solution.py:11
  294.7 2.5 copy-start.30
  (6 other events, 5.6 us)
Sparse Core Ops, SparseCore 0:
  145.0 138.1 all-reduce.28
  285.7 382.0 all-reduce.30
